TPU v7x, 32 devices: a whole 2x2x4 slice. The times are simulated.
32 devices in a mesh: pairs: 8 (over z, y), dom: 4 (over x, core).
Axes of the slice: x: 2, y: 2, z: 4, core: 2. Of those that a mesh axis runs over, the one named last changes fastest.
Arguments:
- amplitude: bfloat16 [64, 384, 384], P('pairs', 'dom'), may hold values from -2 to 2
- integrals: bfloat16 [64, 384, 384], P('pairs', 'dom'), may hold values from -6 to 6
- virtual_energy: float32 [64, 384], P('pairs'), may hold values from 0.2 to 1.5
- occupied_gap: float32 [64], P('pairs'), may hold values from 0.3 to 1.5
- pair_slot: int32 [64], replicated, may hold values from 0 to 63, as said below
- coupling_source: int32 [128], replicated, may hold values from 0 to 63, as said below
- coupling_target: int32 [128], replicated, may hold values from 0 to 63, as said below
- coupling_fock: float32 [128], P(('pairs', 'dom')), may hold values from -3 to 3
- coupling_intersection: bfloat16 [128, 384, 384], P(('pairs', 'dom')), may hold values from -0.3125 to 0.3125
Outputs:
- updated_amplitude: float32 [64, 384, 384], P('pairs', 'dom')
- residual: float32 [64, 384, 384], P('pairs', 'dom')
Inputs may be any that keep to these rules, and one draw needn't show every extreme that they name: A permutation: pair p is stored at position pair_slot[p], which lies on index pair_slot[p] // 8 of pairs. `coupling_target`: coupling c is held by index c // 16 of pairs, and its target pair is stored on that same index; the two couplings that share a source pair on one holder have different targets. `coupling_source`: among the 16 couplings of one holder, every source pair appears in exactly two, and there are 8 distinct source pairs; of the pairs stored on any one index of pairs, a holder uses at most 2 distinct ones as sources, and exactly 2 for some indices on every holder.
All inputs are finite; a program needn't handle non-finite values.
Results may differ from a plain program's by a relative error of at most 0.0024.
Values may be sent and summed in bfloat16 or wider, within the bound.
A program may use at most 128 MiB of HBM per device.

v0:
```python
import jax
import jax.numpy as jnp
from jax import lax
from jax.sharding import PartitionSpec as P

SRC_CAP = 2


def lookup(table, indices):
    places = jnp.arange(table.shape[0], dtype=jnp.int32)
    return jnp.sum(jnp.where(indices[:, None] == places[None, :], table[None, :], 0), axis=1)


def per_device(
    amplitude,
    integrals,
    virtual_energy,
    occupied_gap,
    pair_slot,
    coupling_source,
    coupling_target,
    coupling_fock,
    coupling_intersection,
):
    holders = lax.axis_size("pairs")
    quarters = lax.axis_size("dom")
    own_pair = lax.axis_index("pairs")
    own_quarter = lax.axis_index("dom")
    pair_count, row_count, width = amplitude.shape
    couplings = coupling_source.shape[0] // holders
    quarter_couplings = coupling_intersection.shape[0]
    source_slot = lookup(pair_slot, coupling_source).reshape(holders, couplings)
    target_slot = lookup(pair_slot, coupling_target).reshape(holders, couplings)
    source_owner = source_slot // pair_count
    source_local = source_slot % pair_count
    held_owner = lax.dynamic_index_in_dim(source_owner, own_pair, 0, keepdims=False)
    held_local = lax.dynamic_index_in_dim(source_local, own_pair, 0, keepdims=False)
    held_target = lax.dynamic_index_in_dim(target_slot, own_pair, 0, keepdims=False) % pair_count
    local_numbers = jnp.arange(pair_count, dtype=jnp.int32)
    owner_numbers = jnp.arange(holders, dtype=jnp.int32)
    capacity = SRC_CAP
    wanted = jnp.any(
        (source_owner[:, :, None] == own_pair)
        & (source_local[:, :, None] == local_numbers[None, None, :]),
        axis=1,
    )
    wanted_count = wanted.astype(jnp.int32)
    order = jnp.cumsum(wanted_count, axis=1) - wanted_count
    slot_numbers = jnp.arange(capacity, dtype=jnp.int32)
    chosen = wanted[:, None, :] & (order[:, None, :] == slot_numbers[None, :, None])
    picked = jnp.sum(jnp.where(chosen, local_numbers[None, None, :], 0), axis=2)
    match = (held_owner[:, None, None] == owner_numbers[None, :, None]) & (
        held_local[:, None, None] == local_numbers[None, None, :]
    )
    needed = jnp.any(match, axis=0).astype(jnp.int32)
    held_order = jnp.cumsum(needed, axis=1) - needed
    held_rank = jnp.sum(jnp.where(match, held_order[None], 0), axis=(1, 2))
    held_slot = held_owner * capacity + held_rank
    energy_rows = lax.dynamic_slice_in_dim(virtual_energy, own_quarter * row_count, row_count, 1)
    denominator = energy_rows[:, :, None] + virtual_energy[:, None, :] + occupied_gap[:, None, None]
    target_select = (held_target[None, :] == local_numbers[:, None]).astype(jnp.bfloat16)
    current = amplitude.astype(jnp.float32)
    sent = current.astype(jnp.bfloat16)
    outgoing = jnp.take(sent, picked.reshape(-1), axis=0).reshape(
        holders, capacity, row_count, width
    )
    arrived = lax.all_to_all(outgoing, "pairs", split_axis=0, concat_axis=0, tiled=True)
    held_rows = jnp.take(arrived.reshape(holders * capacity, row_count, width), held_slot, axis=0)
    grouped = held_rows.reshape(quarters, quarter_couplings, row_count, width)
    whole = lax.all_to_all(grouped, "dom", split_axis=0, concat_axis=2, tiled=True).reshape(
        quarter_couplings, quarters * row_count, width
    )
    left = jnp.einsum(
        "cab,cbd->cad", coupling_intersection, whole, preferred_element_type=jnp.float32
    ).astype(jnp.bfloat16)
    projected = jnp.einsum(
        "cad,ced->cae", left, coupling_intersection, preferred_element_type=jnp.float32
    )
    coupled_term = (coupling_fock[:, None, None] * projected).astype(jnp.bfloat16)
    scattered = lax.all_to_all(
        coupled_term.reshape(quarter_couplings, quarters, row_count, width),
        "dom",
        split_axis=1,
        concat_axis=0,
        tiled=True,
    ).reshape(couplings, row_count, width)
    coupled = jnp.einsum(
        "pc,crd->prd", target_select, scattered, preferred_element_type=jnp.float32
    )
    residual = integrals.astype(jnp.float32) + denominator * current - coupled
    current = current - residual / denominator
    return (current, residual)


def solution(mesh):
    in_specs = (
        P("pairs", "dom", None),
        P("pairs", "dom", None),
        P("pairs", None),
        P("pairs"),
        P(),
        P(),
        P(),
        P(("pairs", "dom")),
        P(("pairs", "dom"), None, None),
    )
    out_specs = (P("pairs", "dom", None), P("pairs", "dom", None))
    return jax.shard_map(
        per_device, mesh=mesh, in_specs=in_specs, out_specs=out_specs, check_vma=False
    )
```

profile of v0, /device:TPU:0, one launch (start us, length us, event | category | flops | bytes accessed | tf_op | source)
XLA Modules:
  0.0 88.6 jit_solution(5788474851340077103)
XLA Ops:
  0.7 0.9 select_reduce_fusion.1
  1.5 0.1 reshape.244
  1.6 0.2 fusion.4
  1.9 0.2 reduce_window_sum.18
  2.0 0.2 select_reduce_fusion.2
  2.2 0.1 copy.47
  2.3 0.1 copy.46
  2.4 0.1 reshape.245
  2.5 1.9 %gather_fusion = bf16[16,96,384]{2,1,0:T(8,128)(2,1)S(1)} fusion(bf16[8,96,384]{2,1,0:T(8,128)(2,1)} %param.9, s32[1024]{0:T(1024)S(1)} %pad_clamp_fusion.1), kind=kCustom, calls=%fused_computation | custom fusion | bytes 2359360 | tf_op jit(solution)/shard_map/jit(_take)/gather | solution.py:64
  4.4 1.2 %broadcast_select_fusion = bf16[8,2,96,384]{3,2,1,0:T(8,128)(2,1)} fusion(bf16[8,2,96,384]{3,2,1,0:T(8,128)(2,1)S(1)} %bitcast.39, pred[8,2]{1,0:T(8,128)(4,1)S(1)} %copy.46), kind=kLoop, calls=%fused_computation.10 | loop fusion | flops 589824 | bytes 2359312 | tf_op jit(solution)/shard_map/jit(_take)/select_n | solution.py:64
  5.6 7.3 %all-to-all-start = ((bf16[8,2,96,384]{3,2,1,0:T(8,128)(2,1)}), bf16[8,2,96,384]{3,2,1,0:T(8,128)(2,1)S(1)}, u32[]{:S(2)}, u32[]{:S(2)}) async-start(bf16[8,2,96,384]{3,2,1,0:T(8,128)(2,1)} %broadcast_select_fusion), calls=%async_computation | async-start | bytes 2359296 | tf_op jit(solution)/shard_map/all_to_all | solution.py:67
  12.9 0.1 mul.37
  13.0 0.2 and_reduce_fusion
  13.2 0.2 reduce_window_sum.17
  13.4 0.1 fusion.2
  13.5 0.1 reduce_sum.43
  13.6 27.8 %all-to-all-done = bf16[8,2,96,384]{3,2,1,0:T(8,128)(2,1)S(1)} async-done(((bf16[8,2,96,384]{3,2,1,0:T(8,128)(2,1)}), bf16[8,2,96,384]{3,2,1,0:T(8,128)(2,1)S(1)}, u32[]{:S(2)}, u32[]{:S(2)}) %all-to-all-start) | async-done | bytes 1179680 | tf_op jit(solution)/shard_map/all_to_all | solution.py:67
  41.5 0.8 gather_fusion.1
  42.3 0.2 broadcast_select_fusion.1
  42.5 18.4 %all_to_all.35 = bf16[4,4,96,384]{3,2,1,0:T(8,128)(2,1)S(1)} all-to-all(bf16[4,4,96,384]{3,2,1,0:T(8,128)(2,1)S(1)} %broadcast_select_fusion.1), channel_id=1, replica_groups=mesh['pairs'=8,'dom'=4] {'dom'}, dimensions={0} | all-to-all | bytes 2359296 | tf_op jit(solution)/shard_map/all_to_all | solution.py:70
  60.9 0.1 copy.48
  61.0 0.5 copy-done.3
  61.5 1.8 %multiply_convert_fusion = bf16[4,384,384]{2,1,0:T(8,128)(2,1)S(1)} fusion(bf16[4,384,384]{2,1,0:T(8,128)(2,1)S(1)} %copy-done, bf16[4,384,384]{2,1,0:T(8,128)(2,1)S(1)} %bitcast.42, f32[4]{0:T(128)S(1)} %copy-done.3), kind=kOutput, calls=%fused_computation.2 | convolution fusion | flops 907739136 | bytes 3538960 | tf_op jit(solution)/shard_map/cad,ced->cae/dot_general | solution.py:76
  63.4 1.2 %copy.51 = bf16[4,4,96,384]{3,2,0,1:T(8,128)(2,1)} copy(bf16[4,4,96,384]{3,2,1,0:T(8,128)(2,1)S(1)} %bitcast.43) | data formatting | bytes 2359296 | tf_op jit(solution)/shard_map/reshape | solution.py:81
  64.5 3.7 %all-to-all-start.2 = ((bf16[4,4,96,384]{3,2,0,1:T(8,128)(2,1)}), bf16[4,4,96,384]{3,2,0,1:T(8,128)(2,1)S(1)}, u32[]{:S(2)}, u32[]{:S(2)}) async-start(bf16[4,4,96,384]{3,2,0,1:T(8,128)(2,1)} %copy.51), calls=%async_computation.2 | async-start | bytes 2359296 | tf_op jit(solution)/shard_map/all_to_all | solution.py:80
  68.2 0.1 reshape.243
  68.3 0.1 constant_dynamic-slice_fusion.3
  68.4 0.1 copy.45
  68.5 15.5 %all-to-all-done.2 = bf16[4,4,96,384]{3,2,0,1:T(8,128)(2,1)S(1)} async-done(((bf16[4,4,96,384]{3,2,0,1:T(8,128)(2,1)}), bf16[4,4,96,384]{3,2,0,1:T(8,128)(2,1)S(1)}, u32[]{:S(2)}, u32[]{:S(2)}) %all-to-all-start.2) | async-done | bytes 1179680 | tf_op jit(solution)/shard_map/all_to_all | solution.py:80
  84.0 2.2 %convert_subtract_fusion = (f32[8,96,384]{2,0,1:T(8,128)S(1)}, f32[8,96,384]{2,0,1:T(8,128)S(1)}) fusion(f32[8]{0:T(128)S(1)} %copy-done.4, f32[8,384]{1,0:T(8,128)S(1)} %copy-done.2, f32[8,96]{0,1:T(8,128)S(1)} %copy.45, bf16[8,96,384]{2,1,0:T(8,128)(2,1)S(1)} %copy-done.1, bf16[16,96,384]{2,1,0:T(8,128)(2,1)S(1)} %bitcast.41, s32[16]{0:T(128)S(1)} %fusion.12, ...), kind=kOutput, calls=%fused_computation.4 | convolution fusion | flops 12091520 | bytes 4734048 | tf_op jit(solution)/shard_map/pc,crd->prd/dot_general | solution.py:87
  86.2 1.2 %copy.53 = f32[8,96,384]{2,1,0:T(8,128)} copy(f32[8,96,384]{2,0,1:T(8,128)S(1)} %get-tuple-element.18) | data formatting | bytes 2359296
  87.4 1.2 %copy.54 = f32[8,96,384]{2,1,0:T(8,128)} copy(f32[8,96,384]{2,0,1:T(8,128)S(1)} %get-tuple-element.19) | data formatting | bytes 2359296
  (25 shorter events, 0.2 us)
Async XLA Ops:
  0.6 60.4 %copy-start = (bf16[4,384,384]{2,1,0:T(8,128)(2,1)S(1)}, bf16[4,384,384]{2,1,0:T(8,128)(2,1)}, u32[]{:S(2)}) copy-start(bf16[4,384,384]{2,1,0:T(8,128)(2,1)} %param.17) | copy-start | bytes 3538948
  5.6 35.9 %all-to-all-start = ((bf16[8,2,96,384]{3,2,1,0:T(8,128)(2,1)}), bf16[8,2,96,384]{3,2,1,0:T(8,128)(2,1)S(1)}, u32[]{:S(2)}, u32[]{:S(2)}) async-start(bf16[8,2,96,384]{3,2,1,0:T(8,128)(2,1)} %broadcast_select_fusion), calls=%async_computation | async-start | bytes 2359296 | tf_op jit(solution)/shard_map/all_to_all | solution.py:67
  60.9 0.7 copy-start.3
  64.5 3.8 %copy-start.2 = (f32[8,384]{1,0:T(8,128)S(1)}, f32[8,384]{1,0:T(8,128)}, u32[]{:S(2)}) copy-start(f32[8,384]{1,0:T(8,128)} %param.11) | copy-start | bytes 36868
  64.5 19.5 %copy-start.1 = (bf16[8,96,384]{2,1,0:T(8,128)(2,1)S(1)}, bf16[8,96,384]{2,1,0:T(8,128)(2,1)}, u32[]{:S(2)}) copy-start(bf16[8,96,384]{2,1,0:T(8,128)(2,1)} %param.9) | copy-start | bytes 1769476
  64.5 19.5 %copy-start.4 = (f32[8]{0:T(128)S(1)}, f32[8]{0:T(128)}, u32[]{:S(2)}) copy-start(f32[8]{0:T(128)} %param.12) | copy-start | bytes 100
  64.5 19.5 %all-to-all-start.2 = ((bf16[4,4,96,384]{3,2,0,1:T(8,128)(2,1)}), bf16[4,4,96,384]{3,2,0,1:T(8,128)(2,1)S(1)}, u32[]{:S(2)}, u32[]{:S(2)}) async-start(bf16[4,4,96,384]{3,2,0,1:T(8,128)(2,1)} %copy.51), calls=%async_computation.2 | async-start | bytes 2359296 | tf_op jit(solution)/shard_map/all_to_all | solution.py:80
where the time goes:
time: 89 us; the launch traced here: 88.6 us
  waiting for transfers between devices  43.4 us (49%)
  blocking collectives  18.4 us (21%)
  starting transfers between devices  11 us (12%)
  local copies, waits for them, and re-layouts  7.69 us (9%)
  matrix products  3.99 us (4%)
  other arithmetic  3.46 us (4%)
    all_to_all x1, waiting for transfers between devices, per_device(): lax.all_to_all(outgoing, 'pairs', split_axis=0, concat_axis=0, tiled=True)  27.8 us
    all_to_all x1, blocking collectives, per_device(): lax.all_to_all(grouped, 'dom', split_axis=0, concat_axis=2, tiled=True)  18.4 us
    all_to_all x1, waiting for transfers between devices, per_device(): lax.all_to_all(coupled_term.reshape(quarter_couplings, quarters, row_coun...  15.5 us
    all_to_all x1, starting transfers between devices, per_device(): lax.all_to_all(outgoing, 'pairs', split_axis=0, concat_axis=0, tiled=True)  7.31 us
    all_to_all x1, starting transfers between devices, per_device(): lax.all_to_all(coupled_term.reshape(quarter_couplings, quarters, row_coun...  3.66 us
    unnamed x12, local copies, waits for them, and re-layouts  2.97 us
    dot_general x1, matrix products, per_device(): jnp.einsum('pc,crd->prd', target_select, scattered, preferred_element_typ...  2.16 us
    gather x1, local copies, waits for them, and re-layouts, per_device(): jnp.take(sent, picked.reshape(-1), axis=0)  1.87 us
  transfers between devices with their start and end apart: 2, of which 2 were waited for; matrix products, arithmetic and copies ran while one was open for 1% of the time, Pallas kernels for 0%

commit v1 on v0

--- a/solution.py
+++ b/solution.py
@@ -4,6 +4,18 @@
 from jax.sharding import PartitionSpec as P
 
 SRC_CAP = 2
+
+
+def cut_along(array, dim, count):
+    shape = array.shape
+    blocks = array.reshape(*shape[:dim], count, shape[dim] // count, *shape[dim + 1 :])
+    return jnp.moveaxis(blocks, dim, 0)
+
+
+def in_order(tiles, dim):
+    tiles = jnp.moveaxis(tiles, 0, dim)
+    shape = tiles.shape
+    return tiles.reshape(*shape[:dim], shape[dim] * shape[dim + 1], *shape[dim + 2 :])
 
 
 def lookup(table, indices):
@@ -64,7 +76,14 @@
     outgoing = jnp.take(sent, picked.reshape(-1), axis=0).reshape(
         holders, capacity, row_count, width
     )
-    arrived = lax.all_to_all(outgoing, "pairs", split_axis=0, concat_axis=0, tiled=True)
+    size, index = (lax.axis_size("pairs"), lax.axis_index("pairs"))
+    parts = cut_along(outgoing, 0, size)
+    outs = [parts[index]]
+    for step in range(1, size):
+        sent_2 = parts[index ^ step]
+        outs.append(lax.ppermute(sent_2, "pairs", [(i, i ^ step) for i in range(size)]))
+    parts = jnp.stack(outs)[index ^ jnp.arange(size)]
+    arrived = in_order(parts, 0)
     held_rows = jnp.take(arrived.reshape(holders * capacity, row_count, width), held_slot, axis=0)
     grouped = held_rows.reshape(quarters, quarter_couplings, row_count, width)
     whole = lax.all_to_all(grouped, "dom", split_axis=0, concat_axis=2, tiled=True).reshape(

time: 89 us -> 90.6 us (1.018)
  waiting for transfers between devices: 43.4 us -> 30.4 us
  starting transfers between devices: 11 us -> 21.2 us
  local copies, waits for them, and re-layouts: 7.69 us -> 12.5 us
    all_to_all x1 -> x0, waiting for transfers between devices: 27.8 us -> none  [per_device(): lax.all_to_all(outgoing, 'pairs', split_axis=0, concat_axis=0, tiled=True)]
    ppermute x0 -> x7, starting transfers between devices: none -> 17.5 us  [per_device(): lax.ppermute(sent_2, 'pairs', [(i, i ^ step) for i in range(size)])]
    ppermute x0 -> x7, waiting for transfers between devices: none -> 14.9 us  [per_device(): lax.ppermute(sent_2, 'pairs', [(i, i ^ step) for i in range(size)])]
    all_to_all x1 -> x0, starting transfers between devices: 7.31 us -> none  [per_device(): lax.all_to_all(outgoing, 'pairs', split_axis=0, concat_axis=0, tiled=True)]
    unnamed x12 -> x20, local copies, waits for them, and re-layouts: 2.97 us -> 6.77 us
    select_n x2, other arithmetic: 1.22 us -> 0.21 us  [per_device(): jnp.take(sent, picked.reshape(-1), axis=0)]
  transfers between devices with their start and end apart: 2 -> 8, of which waited for: 2 -> 4; matrix products, arithmetic and copies ran while one was open for 1% -> 5% of each run, Pallas kernels for 0% -> 0%
where the time goes in v1:
time: 90.6 us; the launch traced here: 90.2 us
  waiting for transfers between devices  30.4 us (34%)
  starting transfers between devices  21.2 us (23%)
  blocking collectives  18.4 us (20%)
  local copies, waits for them, and re-layouts  12.5 us (14%)
  matrix products  3.78 us (4%)
  other arithmetic  2.96 us (3%)
  between operations  0.94 us (1%)
    all_to_all x1, blocking collectives, per_device(): lax.all_to_all(grouped, 'dom', split_axis=0, concat_axis=2, tiled=True)  18.4 us
    ppermute x7, starting transfers between devices, per_device(): lax.ppermute(sent_2, 'pairs', [(i, i ^ step) for i in range(size)])  17.5 us
    all_to_all x1, waiting for transfers between devices, per_device(): lax.all_to_all(coupled_term.reshape(quarter_couplings, quarters, row_coun...  15.5 us
    ppermute x7, waiting for transfers between devices, per_device(): lax.ppermute(sent_2, 'pairs', [(i, i ^ step) for i in range(size)])  14.9 us
    unnamed x20, local copies, waits for them, and re-layouts  6.77 us
    all_to_all x1, starting transfers between devices, per_device(): lax.all_to_all(coupled_term.reshape(quarter_couplings, quarters, row_coun...  3.67 us
    dot_general x1, matrix products, per_device(): jnp.einsum('pc,crd->prd', target_select, scattered, preferred_element_typ...  1.98 us
    gather x1, local copies, waits for them, and re-layouts, per_device(): jnp.take(sent, picked.reshape(-1), axis=0)  1.87 us
  transfers between devices with their start and end apart: 8, of which 4 were waited for; matrix products, arithmetic and copies ran while one was open for 5% of the time, Pallas kernels for 0%

profile of v1, /device:TPU:0, one launch (start us, length us, event | category | flops | bytes accessed | tf_op | source)
XLA Modules:
  0.0 90.2 jit_solution(15913262224274623537)
XLA Ops:
  0.7 1.4 %select_reduce_fusion.1 = (s32[128]{0:T(128)}, s32[128]{0:T(128)S(1)}) fusion(s32[64]{0:T(128)} %param.13, s32[128]{0:T(128)} %param.15, s32[128]{0:T(128)} %param.14), kind=kLoop, calls=%fused_computation.34 | loop fusion | flops 48896 | bytes 2304 | tf_op jit(solution)/shard_map/reduce_sum | solution.py:23
  2.2 0.2 fusion.4
  2.4 0.2 reduce_window_sum.18
  2.9 0.2 and_reduce_fusion
  3.6 1.9 %gather_fusion = bf16[16,96,384]{2,1,0:T(8,128)(2,1)S(1)} fusion(bf16[8,96,384]{2,1,0:T(8,128)(2,1)} %param.9, s32[1024]{0:T(1024)S(1)} %get-tuple-element.29), kind=kCustom, calls=%fused_computation | custom fusion | bytes 2359360 | tf_op jit(solution)/shard_map/jit(_take)/gather | solution.py:76
  5.5 0.2 broadcast_select_fusion
  5.9 6.1 %collective-permute-start.6 = (bf16[1,2,96,384]{3,2,1,0:T(8,128)(2,1)S(1)}, bf16[1,2,96,384]{3,2,1,0:T(8,128)(2,1)S(1)}, u32[]{:S(2)}, u32[]{:S(2)}) collective-permute-start(bf16[1,2,96,384]{3,2,1,0:T(8,128)(2,1)S(1)} %get-tuple-element.16), channel_id=1, source_target_pairs={{0,28},{4,24},{8,20},{12,16},{16,12},{20,8},{24,4},{28,0},{1,29},{... | collective-permute-start | bytes 442376 | tf_op jit(solution)/shard_map/ppermute | solution.py:84
  12.0 0.2 collective-permute-start.5
  12.2 0.7 collective-permute-start.4
  12.9 2.0 %collective-permute-start.3 = (bf16[1,2,96,384]{3,2,1,0:T(8,128)(2,1)S(1)}, bf16[1,2,96,384]{3,2,1,0:T(8,128)(2,1)}, u32[]{:S(2)}, u32[]{:S(2)}) collective-permute-start(bf16[1,2,96,384]{3,2,1,0:T(8,128)(2,1)S(1)} %get-tuple-element.19), channel_id=1, source_target_pairs={{0,16},{4,20},{8,24},{12,28},{16,0},{20,4},{24,8},{28,12},{1,17},{... | collective-permute-start | bytes 442376 | tf_op jit(solution)/shard_map/ppermute | solution.py:84
  15.0 1.6 %collective-permute-start = (bf16[1,2,96,384]{3,2,1,0:T(8,128)(2,1)S(1)}, bf16[1,2,96,384]{3,2,1,0:T(8,128)(2,1)}, u32[]{:S(2)}, u32[]{:S(2)}) collective-permute-start(bf16[1,2,96,384]{3,2,1,0:T(8,128)(2,1)S(1)} %get-tuple-element.22), channel_id=1, source_target_pairs={{0,4},{4,0},{8,12},{12,8},{16,20},{20,16},{24,28},{28,24},{1,5},{5... | collective-permute-start | bytes 442376 | tf_op jit(solution)/shard_map/ppermute | solution.py:84
  16.8 3.4 %collective-permute-done = bf16[1,2,96,384]{3,2,1,0:T(8,128)(2,1)} collective-permute-done((bf16[1,2,96,384]{3,2,1,0:T(8,128)(2,1)S(1)}, bf16[1,2,96,384]{3,2,1,0:T(8,128)(2,1)}, u32[]{:S(2)}, u32[]{:S(2)}) %collective-permute-start) | collective-permute-done | bytes 147488 | tf_op jit(solution)/shard_map/ppermute | solution.py:84
  20.2 4.2 %collective-permute-start.1 = (bf16[1,2,96,384]{3,2,1,0:T(8,128)(2,1)S(1)}, bf16[1,2,96,384]{3,2,1,0:T(8,128)(2,1)S(1)}, u32[]{:S(2)}, u32[]{:S(2)}) collective-permute-start(bf16[1,2,96,384]{3,2,1,0:T(8,128)(2,1)S(1)} %get-tuple-element.21), channel_id=1, source_target_pairs={{0,8},{4,12},{8,0},{12,4},{16,24},{20,28},{24,16},{28,20},{1,9},{5... | collective-permute-start | bytes 442376 | tf_op jit(solution)/shard_map/ppermute | solution.py:84
  24.4 0.9 %bitcast_dynamic-update-slice_fusion.6 = bf16[8,1,2,96,384]{4,3,2,0,1:T(8,128)(2,1)S(1)} fusion(bf16[8,1,2,96,384]{4,3,2,0,1:T(8,128)(2,1)S(1)} %get-tuple-element.23, bf16[1,2,96,384]{3,2,1,0:T(8,128)(2,1)} %collective-permute-done), kind=kLoop, calls=%fused_computation.19 | loop fusion | bytes 294912
  25.3 2.5 %collective-permute-done.1 = bf16[1,2,96,384]{3,2,1,0:T(8,128)(2,1)S(1)} collective-permute-done((bf16[1,2,96,384]{3,2,1,0:T(8,128)(2,1)S(1)}, bf16[1,2,96,384]{3,2,1,0:T(8,128)(2,1)S(1)}, u32[]{:S(2)}, u32[]{:S(2)}) %collective-permute-start.1) | collective-permute-done | bytes 147488 | tf_op jit(solution)/shard_map/ppermute | solution.py:84
  27.8 2.7 %collective-permute-start.2 = (bf16[1,2,96,384]{3,2,1,0:T(8,128)(2,1)S(1)}, bf16[1,2,96,384]{3,2,1,0:T(8,128)(2,1)S(1)}, u32[]{:S(2)}, u32[]{:S(2)}) collective-permute-start(bf16[1,2,96,384]{3,2,1,0:T(8,128)(2,1)S(1)} %get-tuple-element.20), channel_id=1, source_target_pairs={{0,12},{4,8},{8,4},{12,0},{16,28},{20,24},{24,20},{28,16},{1,13},{... | collective-permute-start | bytes 442376 | tf_op jit(solution)/shard_map/ppermute | solution.py:84
  30.4 9.0 %collective-permute-done.2 = bf16[1,2,96,384]{3,2,1,0:T(8,128)(2,1)S(1)} collective-permute-done((bf16[1,2,96,384]{3,2,1,0:T(8,128)(2,1)S(1)}, bf16[1,2,96,384]{3,2,1,0:T(8,128)(2,1)S(1)}, u32[]{:S(2)}, u32[]{:S(2)}) %collective-permute-start.2) | collective-permute-done | bytes 147488 | tf_op jit(solution)/shard_map/ppermute | solution.py:84
  39.5 0.9 %bitcast_dynamic-update-slice_fusion.3 = bf16[8,1,2,96,384]{4,3,2,0,1:T(8,128)(2,1)S(1)} fusion(bf16[8,1,2,96,384]{4,3,2,0,1:T(8,128)(2,1)S(1)} %bitcast_dynamic-update-slice_fusion.4, bf16[1,2,96,384]{3,2,1,0:T(8,128)(2,1)} %collective-permute-done.3), kind=kLoop, calls=%fused_computation.16 | loop fusion | bytes 294912
  40.4 0.9 %bitcast_dynamic-update-slice_fusion.2 = bf16[8,1,2,96,384]{4,3,2,0,1:T(8,128)(2,1)S(1)} fusion(bf16[8,1,2,96,384]{4,3,2,0,1:T(8,128)(2,1)S(1)} %bitcast_dynamic-update-slice_fusion.3, bf16[1,2,96,384]{3,2,1,0:T(8,128)(2,1)} %collective-permute-done.4), kind=kLoop, calls=%fused_computation.15 | loop fusion | bytes 294912
  41.4 0.9 %bitcast_dynamic-update-slice_fusion.1 = bf16[8,1,2,96,384]{4,3,2,0,1:T(8,128)(2,1)S(1)} fusion(bf16[8,1,2,96,384]{4,3,2,0,1:T(8,128)(2,1)S(1)} %bitcast_dynamic-update-slice_fusion.2, bf16[1,2,96,384]{3,2,1,0:T(8,128)(2,1)} %collective-permute-done.5), kind=kLoop, calls=%fused_computation.14 | loop fusion | bytes 294912
  42.4 0.8 gather_fusion.1
  43.2 0.8 gather_fusion.2
  44.0 0.2 broadcast_select_fusion.1
  44.2 18.4 %all_to_all.30 = bf16[4,4,96,384]{3,2,1,0:T(8,128)(2,1)S(1)} all-to-all(bf16[4,4,96,384]{3,2,1,0:T(8,128)(2,1)S(1)} %broadcast_select_fusion.1), channel_id=1, replica_groups=mesh['pairs'=8,'dom'=4] {'dom'}, dimensions={0} | all-to-all | bytes 2359296 | tf_op jit(solution)/shard_map/all_to_all | solution.py:89
  62.8 0.5 copy-done.4
  63.3 1.8 %multiply_convert_fusion = bf16[4,384,384]{2,1,0:T(8,128)(2,1)S(1)} fusion(bf16[4,384,384]{2,1,0:T(8,128)(2,1)S(1)} %copy-done, bf16[4,384,384]{2,1,0:T(8,128)(2,1)S(1)} %bitcast.74, f32[4]{0:T(128)S(1)} %copy-done.4), kind=kOutput, calls=%fused_computation.3 | convolution fusion | flops 907739136 | bytes 3538960 | tf_op jit(solution)/shard_map/cad,ced->cae/dot_general | solution.py:95
  65.1 1.2 %copy.51 = bf16[4,4,96,384]{3,2,0,1:T(8,128)(2,1)} copy(bf16[4,4,96,384]{3,2,1,0:T(8,128)(2,1)S(1)} %bitcast.75) | data formatting | bytes 2359296 | tf_op jit(solution)/shard_map/reshape | solution.py:100
  66.2 3.7 %all-to-all-start.1 = ((bf16[4,4,96,384]{3,2,0,1:T(8,128)(2,1)}), bf16[4,4,96,384]{3,2,0,1:T(8,128)(2,1)S(1)}, u32[]{:S(2)}, u32[]{:S(2)}) async-start(bf16[4,4,96,384]{3,2,0,1:T(8,128)(2,1)} %copy.51), calls=%async_computation.1 | async-start | bytes 2359296 | tf_op jit(solution)/shard_map/all_to_all | solution.py:99
  70.2 15.5 %all-to-all-done.1 = bf16[4,4,96,384]{3,2,0,1:T(8,128)(2,1)S(1)} async-done(((bf16[4,4,96,384]{3,2,0,1:T(8,128)(2,1)}), bf16[4,4,96,384]{3,2,0,1:T(8,128)(2,1)S(1)}, u32[]{:S(2)}, u32[]{:S(2)}) %all-to-all-start.1) | async-done | bytes 1179680 | tf_op jit(solution)/shard_map/all_to_all | solution.py:99
  85.7 2.0 %convert_subtract_fusion = (f32[8,96,384]{2,0,1:T(8,128)S(1)}, f32[8,96,384]{2,0,1:T(8,128)S(1)}) fusion(f32[8]{0:T(128)S(1)} %copy-done.5, f32[8,384]{1,0:T(8,128)S(1)} %copy-done.3, f32[8,96]{0,1:T(8,128)S(1)} %copy.45, bf16[8,96,384]{2,1,0:T(8,128)(2,1)S(1)} %copy-done.1, bf16[16,96,384]{2,1,0:T(8,128)(2,1)S(1)} %bitcast.73, s32[16]{0:T(128)S(1)} %fusion.11, ...), kind=kOutput, calls=%fused_computation.5 | convolution fusion | flops 12091520 | bytes 4734048 | tf_op jit(solution)/shard_map/pc,crd->prd/dot_general | solution.py:106
  87.7 1.2 %copy.53 = f32[8,96,384]{2,1,0:T(8,128)} copy(f32[8,96,384]{2,0,1:T(8,128)S(1)} %get-tuple-element.26) | data formatting | bytes 2359296
  88.9 1.2 %copy.54 = f32[8,96,384]{2,1,0:T(8,128)} copy(f32[8,96,384]{2,0,1:T(8,128)S(1)} %get-tuple-element.27) | data formatting | bytes 2359296
  (50 shorter events, 1.7 us)
Async XLA Ops:
  0.6 62.1 %copy-start = (bf16[4,384,384]{2,1,0:T(8,128)(2,1)S(1)}, bf16[4,384,384]{2,1,0:T(8,128)(2,1)}, u32[]{:S(2)}) copy-start(bf16[4,384,384]{2,1,0:T(8,128)(2,1)} %param.17) | copy-start | bytes 3538948
  5.9 36.5 %collective-permute-start.6 = (bf16[1,2,96,384]{3,2,1,0:T(8,128)(2,1)S(1)}, bf16[1,2,96,384]{3,2,1,0:T(8,128)(2,1)S(1)}, u32[]{:S(2)}, u32[]{:S(2)}) collective-permute-start(bf16[1,2,96,384]{3,2,1,0:T(8,128)(2,1)S(1)} %get-tuple-element.16), channel_id=1, source_target_pairs={{0,28},{4,24},{8,20},{12,16},{16,12},{20,8},{24,4},{28,0},{1,29},{... | collective-permute-start | bytes 442376 | tf_op jit(solution)/shard_map/ppermute | solution.py:84
  12.0 29.4 %collective-permute-start.5 = (bf16[1,2,96,384]{3,2,1,0:T(8,128)(2,1)S(1)}, bf16[1,2,96,384]{3,2,1,0:T(8,128)(2,1)}, u32[]{:S(2)}, u32[]{:S(2)}) collective-permute-start(bf16[1,2,96,384]{3,2,1,0:T(8,128)(2,1)S(1)} %get-tuple-element.17), channel_id=1, source_target_pairs={{0,24},{4,28},{8,16},{12,20},{16,8},{20,12},{24,0},{28,4},{1,25},{... | collective-permute-start | bytes 442376 | tf_op jit(solution)/shard_map/ppermute | solution.py:84
  12.2 28.3 %collective-permute-start.4 = (bf16[1,2,96,384]{3,2,1,0:T(8,128)(2,1)S(1)}, bf16[1,2,96,384]{3,2,1,0:T(8,128)(2,1)}, u32[]{:S(2)}, u32[]{:S(2)}) collective-permute-start(bf16[1,2,96,384]{3,2,1,0:T(8,128)(2,1)S(1)} %get-tuple-element.18), channel_id=1, source_target_pairs={{0,20},{4,16},{8,28},{12,24},{16,4},{20,0},{24,12},{28,8},{1,21},{... | collective-permute-start | bytes 442376 | tf_op jit(solution)/shard_map/ppermute | solution.py:84
  12.9 26.6 %collective-permute-start.3 = (bf16[1,2,96,384]{3,2,1,0:T(8,128)(2,1)S(1)}, bf16[1,2,96,384]{3,2,1,0:T(8,128)(2,1)}, u32[]{:S(2)}, u32[]{:S(2)}) collective-permute-start(bf16[1,2,96,384]{3,2,1,0:T(8,128)(2,1)S(1)} %get-tuple-element.19), channel_id=1, source_target_pairs={{0,16},{4,20},{8,24},{12,28},{16,0},{20,4},{24,8},{28,12},{1,17},{... | collective-permute-start | bytes 442376 | tf_op jit(solution)/shard_map/ppermute | solution.py:84
  15.0 5.2 %collective-permute-start = (bf16[1,2,96,384]{3,2,1,0:T(8,128)(2,1)S(1)}, bf16[1,2,96,384]{3,2,1,0:T(8,128)(2,1)}, u32[]{:S(2)}, u32[]{:S(2)}) collective-permute-start(bf16[1,2,96,384]{3,2,1,0:T(8,128)(2,1)S(1)} %get-tuple-element.22), channel_id=1, source_target_pairs={{0,4},{4,0},{8,12},{12,8},{16,20},{20,16},{24,28},{28,24},{1,5},{5... | collective-permute-start | bytes 442376 | tf_op jit(solution)/shard_map/ppermute | solution.py:84
  20.2 7.5 %collective-permute-start.1 = (bf16[1,2,96,384]{3,2,1,0:T(8,128)(2,1)S(1)}, bf16[1,2,96,384]{3,2,1,0:T(8,128)(2,1)S(1)}, u32[]{:S(2)}, u32[]{:S(2)}) collective-permute-start(bf16[1,2,96,384]{3,2,1,0:T(8,128)(2,1)S(1)} %get-tuple-element.21), channel_id=1, source_target_pairs={{0,8},{4,12},{8,0},{12,4},{16,24},{20,28},{24,16},{28,20},{1,9},{5... | collective-permute-start | bytes 442376 | tf_op jit(solution)/shard_map/ppermute | solution.py:84
  27.8 11.7 %collective-permute-start.2 = (bf16[1,2,96,384]{3,2,1,0:T(8,128)(2,1)S(1)}, bf16[1,2,96,384]{3,2,1,0:T(8,128)(2,1)S(1)}, u32[]{:S(2)}, u32[]{:S(2)}) collective-permute-start(bf16[1,2,96,384]{3,2,1,0:T(8,128)(2,1)S(1)} %get-tuple-element.20), channel_id=1, source_target_pairs={{0,12},{4,8},{8,4},{12,0},{16,28},{20,24},{24,20},{28,16},{1,13},{... | collective-permute-start | bytes 442376 | tf_op jit(solution)/shard_map/ppermute | solution.py:84
  62.6 0.7 copy-start.4
  66.2 3.7 %copy-start.2 = (s32[128]{0:T(128)S(1)}, s32[128]{0:T(128)}, u32[]{:S(2)}) copy-start(s32[128]{0:T(128)} %get-tuple-element.12) | copy-start | bytes 1540
  66.2 3.8 %copy-start.3 = (f32[8,384]{1,0:T(8,128)S(1)}, f32[8,384]{1,0:T(8,128)}, u32[]{:S(2)}) copy-start(f32[8,384]{1,0:T(8,128)} %param.11) | copy-start | bytes 36868
  66.2 19.5 %copy-start.1 = (bf16[8,96,384]{2,1,0:T(8,128)(2,1)S(1)}, bf16[8,96,384]{2,1,0:T(8,128)(2,1)}, u32[]{:S(2)}) copy-start(bf16[8,96,384]{2,1,0:T(8,128)(2,1)} %param.9) | copy-start | bytes 1769476
  66.2 19.5 %copy-start.5 = (f32[8]{0:T(128)S(1)}, f32[8]{0:T(128)}, u32[]{:S(2)}) copy-start(f32[8]{0:T(128)} %param.12) | copy-start | bytes 100
  66.2 19.5 %all-to-all-start.1 = ((bf16[4,4,96,384]{3,2,0,1:T(8,128)(2,1)}), bf16[4,4,96,384]{3,2,0,1:T(8,128)(2,1)S(1)}, u32[]{:S(2)}, u32[]{:S(2)}) async-start(bf16[4,4,96,384]{3,2,0,1:T(8,128)(2,1)} %copy.51), calls=%async_computation.1 | async-start | bytes 2359296 | tf_op jit(solution)/shard_map/all_to_all | solution.py:99
